TPU v7x, 512 devices: a whole 4x4x16 slice. The times are simulated.
512 devices in a mesh: ent: 128 (over z, y, core), rep: 4 (over x).
Axes of the slice: x: 4, y: 4, z: 16, core: 2. Of those that a mesh axis runs over, the one named last changes fastest.
Arguments:
- entity_table: float32 [65536, 400], P('ent'), may hold values from -1.8 to 1.8
- adagrad_state: float32 [65536], P('ent'), may hold values from 0.05 to 0.5
- head_owner: int32 [65536, 1], P(('ent', 'rep')), may hold values from 0 to 127; in each aligned block of 128 rows (0 to 127, 128 to 255, ...) at most 2 rows name the same one
- head_row: int32 [65536], P(('ent', 'rep')), may hold values from 0 to 511
- relation_ids: int32 [65536], P(('ent', 'rep')), may hold values from 0 to 63
- tail_owner: int32 [65536, 1], P(('ent', 'rep')), may hold values from 0 to 127; in each aligned block of 128 rows (0 to 127, 128 to 255, ...) at most 2 rows name the same one
- tail_row: int32 [65536], P(('ent', 'rep')), may hold values from 0 to 511
- neg_rows: int32 [512], P('ent'), may hold values from 0 to 511
- relations: float32 [64, 400], replicated, may hold values from -6 to 6
Outputs:
- table_new: float32 [65536, 400], P('ent')
- state_new: float32 [65536], P('ent')
Inputs may be any that keep to these rules, and one draw needn't show every extreme that they name: `head_owner`: among the 128 rows of one device no owner is named more than 2 times; in some device one owner is named exactly 2 times. `tail_owner`: among the 128 rows of one device no owner is named more than 2 times; in some device one owner is named exactly 2 times.
All inputs are finite; a program needn't handle non-finite values.
Results may differ from a plain program's by a relative error of at most 0.0001.
Values sent between devices are 32-bit elements; how exact they have to be, the bound alone decides.
No kernel may reach another device: no remote copies, remote signals or barrier semaphores. Data moves between devices by JAX's collectives and lax.ppermute only.
A program may use at most 64 MiB of HBM per device.

v0:
```python
import math
import jax
import jax.numpy as jnp
from jax import lax
from jax.sharding import PartitionSpec as P

learn_rate = 0.1


def complex_mul(left_re, left_im, right_re, right_im):
    return (left_re * right_re - left_im * right_im, left_re * right_im + left_im * right_re)


def edge_terms(heads, tails, rel_vecs, negatives):
    half = heads.shape[1] // 2
    head_re, head_im = (heads[:, :half], heads[:, half:])
    tail_re, tail_im = (tails[:, :half], tails[:, half:])
    rel_re, rel_im = (rel_vecs[:, :half], rel_vecs[:, half:])
    query = jnp.concatenate(complex_mul(head_re, head_im, rel_re, rel_im), 1)
    probe = jnp.concatenate(complex_mul(rel_re, -rel_im, tail_re, tail_im), 1)
    pos_score = jnp.sum(heads * probe, 1)
    dims = (((1,), (1,)), ((), ()))
    tail_scores = lax.dot_general(query, negatives, dims, precision=lax.Precision.HIGHEST)
    head_scores = lax.dot_general(probe, negatives, dims, precision=lax.Precision.HIGHEST)
    neg_weight = 1.0 / math.sqrt(negatives.shape[0])
    tail_coef = jax.nn.sigmoid(tail_scores) * neg_weight
    head_coef = jax.nn.sigmoid(head_scores) * neg_weight
    pos_coef = -jax.nn.sigmoid(-pos_score)[:, None]
    query_grad = jnp.dot(tail_coef, negatives, precision=lax.Precision.HIGHEST)
    probe_grad = jnp.dot(head_coef, negatives, precision=lax.Precision.HIGHEST)
    head_grad = pos_coef * probe + jnp.concatenate(
        complex_mul(query_grad[:, :half], query_grad[:, half:], rel_re, -rel_im), 1
    )
    tail_grad = pos_coef * query + jnp.concatenate(
        complex_mul(probe_grad[:, :half], probe_grad[:, half:], rel_re, rel_im), 1
    )
    back = (((0,), (0,)), ((), ()))
    negs_grad = lax.dot_general(tail_coef, query, back, precision=lax.Precision.HIGHEST)
    negs_grad = negs_grad + lax.dot_general(head_coef, probe, back, precision=lax.Precision.HIGHEST)
    return (head_grad, tail_grad, negs_grad)


def slot_rank(owners, owners_count):
    member = (owners[:, None] == jnp.arange(owners_count, dtype=jnp.int32)[None, :]).astype(
        jnp.int32
    )
    return jnp.sum(jnp.cumsum(member, 0) * member, 1) - 1


def fetch_single(asks, entity_table):
    received = lax.all_to_all(asks, "ent", split_axis=0, concat_axis=0, tiled=True)
    found = entity_table[received]
    returned = lax.all_to_all(found, "ent", split_axis=0, concat_axis=0, tiled=True)
    return (returned, received)


def on_device(
    entity_table,
    adagrad_state,
    head_owner,
    head_row,
    relation_ids,
    tail_owner,
    tail_row,
    neg_rows,
    relations,
):
    owners_count = lax.axis_size("ent")
    edge_count = head_row.shape[0]
    capacity = max(2, 3 * edge_count // (2 * owners_count))
    width = entity_table.shape[1]
    head_dest = head_owner[:, 0]
    tail_dest = tail_owner[:, 0]
    head_slot = slot_rank(head_dest, owners_count)
    tail_slot = slot_rank(tail_dest, owners_count)
    head_asks = (
        jnp.zeros((owners_count, capacity), jnp.int32).at[head_dest, head_slot].set(head_row)
    )
    tail_asks = (
        jnp.zeros((owners_count, capacity), jnp.int32).at[tail_dest, tail_slot].set(tail_row)
    )
    head_back, head_recv = fetch_single(head_asks, entity_table)
    tail_back, tail_recv = fetch_single(tail_asks, entity_table)
    negatives = lax.all_gather(entity_table[neg_rows], "ent", axis=0, tiled=True)
    heads = head_back[head_dest, head_slot]
    tails = tail_back[tail_dest, tail_slot]
    relation_pick = (
        relation_ids[:, None] == jnp.arange(relations.shape[0], dtype=jnp.int32)[None, :]
    ).astype(jnp.float32)
    rel_vecs = jnp.dot(relation_pick, relations, precision=lax.Precision.HIGHEST)
    head_grad, tail_grad, negs_grad = edge_terms(heads, tails, rel_vecs, negatives)
    head_buffer = (
        jnp.zeros((owners_count, capacity, width), jnp.float32)
        .at[head_dest, head_slot]
        .set(head_grad)
    )
    tail_buffer = (
        jnp.zeros((owners_count, capacity, width), jnp.float32)
        .at[tail_dest, tail_slot]
        .set(tail_grad)
    )
    head_home, tail_home = (
        lax.all_to_all(head_buffer, "ent", split_axis=0, concat_axis=0, tiled=True),
        lax.all_to_all(tail_buffer, "ent", split_axis=0, concat_axis=0, tiled=True),
    )
    grad_table = (
        jnp.zeros_like(entity_table).at[head_recv].add(head_home).at[tail_recv].add(tail_home)
    )
    owned_negs = lax.psum_scatter(negs_grad, "ent", scatter_dimension=0, tiled=True)
    grad_table = grad_table.at[neg_rows].add(owned_negs)
    total_grad = lax.psum(grad_table, "rep")
    state_new = adagrad_state + jnp.mean(total_grad * total_grad, 1)
    table_new = entity_table - learn_rate * total_grad / jnp.sqrt(state_new)[:, None]
    return (table_new, state_new)


def solution(mesh):
    placed = (
        P("ent", None),
        P("ent"),
        P(("ent", "rep"), None),
        P(("ent", "rep")),
        P(("ent", "rep")),
        P(("ent", "rep"), None),
        P(("ent", "rep")),
        P("ent"),
        P(),
    )
    return jax.shard_map(
        on_device, mesh=mesh, in_specs=placed, out_specs=(P("ent", None), P("ent")), check_vma=False
    )
```

profile of v0, /device:TPU:8, one launch (start us, length us, event | category | flops | bytes accessed | tf_op | source)
XLA Modules:
  0.0 747.2 jit_solution(8857684919178705889)
XLA Ops:
  7.2 0.7 copy-done.9
  8.0 0.2 reduce_window_sum.18
  8.1 0.2 select_reduce_fusion
  8.4 0.3 copy-done.12
  8.6 6.4 scatter_fusion.1
  15.0 0.7 copy.35
  15.7 19.5 %all-to-all-start.2 = ((s32[128,1,2]{2,1,0:T(1,128)}), s32[128,1,2]{2,1,0:T(1,128)S(1)}, u32[]{:S(2)}, u32[]{:S(2)}) async-start(s32[128,1,2]{2,1,0:T(1,128)} %copy.35), calls=%async_computation.2 | async-start | bytes 131072 | tf_op jit(solution)/shard_map/all_to_all | solution.py:51
  35.3 0.6 copy-done.10
  36.0 0.2 reduce_window_sum.17
  36.2 0.2 select_reduce_fusion.1
  36.4 0.3 copy.45
  36.7 0.6 copy-done.13
  37.4 6.4 scatter_fusion
  43.7 0.7 copy.33
  44.5 4.6 all-to-all-done.2
  49.1 11.5 %all-to-all-start = ((s32[128,1,2]{2,1,0:T(1,128)}), s32[128,1,2]{2,1,0:T(1,128)S(1)}, u32[]{:S(2)}, u32[]{:S(2)}) async-start(s32[128,1,2]{2,1,0:T(1,128)} %copy.33), calls=%async_computation | async-start | bytes 131072 | tf_op jit(solution)/shard_map/all_to_all | solution.py:51
  60.6 0.1 reshape.129
  60.8 1.0 gather_fusion.2
  61.7 1.1 reshape.128
  62.9 11.6 %all-to-all-done = s32[128,1,2]{2,1,0:T(1,128)S(1)} async-done(((s32[128,1,2]{2,1,0:T(1,128)}), s32[128,1,2]{2,1,0:T(1,128)S(1)}, u32[]{:S(2)}, u32[]{:S(2)}) %all-to-all-start) | async-done | bytes 1056 | tf_op jit(solution)/shard_map/all_to_all | solution.py:51
  74.4 6.7 all-to-all-start.3
  81.2 0.1 reshape.169
  81.3 1.0 gather_fusion
  82.3 1.2 reshape.114
  83.4 29.2 %all-to-all-done.3 = f32[128,2,400]{2,1,0:T(2,128)S(1)} async-done(((f32[128,2,400]{2,1,0:T(2,128)}), f32[128,2,400]{2,1,0:T(2,128)S(1)}, u32[]{:S(2)}, u32[]{:S(2)}) %all-to-all-start.3) | async-done | bytes 409632 | tf_op jit(solution)/shard_map/all_to_all | solution.py:53
  112.6 8.6 %all-to-all-start.1 = ((f32[128,2,400]{2,1,0:T(2,128)}), f32[128,2,400]{2,1,0:T(2,128)S(1)}, u32[]{:S(2)}, u32[]{:S(2)}) async-start(f32[128,2,400]{2,1,0:T(2,128)} %reshape.114), calls=%async_computation.1 | async-start | bytes 1048576 | tf_op jit(solution)/shard_map/all_to_all | solution.py:53
  121.2 0.6 gather_fusion.4
  121.8 127.3 %all-gather.1 = f32[128,4,400]{2,1,0:T(4,128)} all-gather(f32[1,4,400]{2,1,0:T(4,128)S(1)} %bitcast.61), channel_id=2, replica_groups=mesh['ent'=128,'rep'=4] {'ent'}, dimensions={0}, use_global_device_ids=true | all-gather | bytes 825600 | tf_op jit(solution)/shard_map/all_gather | solution.py:84
  249.1 1.6 reshape.205
  250.8 0.4 fusion.13
  251.2 1.8 gather_fusion.3
  252.9 1.1 fusion.28
  254.1 0.7 copy.47
  254.9 1.8 gather_fusion.1
  256.6 1.1 copy.39
  257.9 1.3 fusion.7
  259.2 1.8 fusion.30
  261.0 1.3 fusion.4
  262.3 1.8 fusion.29
  264.3 0.1 copy.43
  264.5 0.9 broadcast.142.clone
  265.4 16.1 %scatter_fusion.2 = f32[128,2,400]{2,1,0:T(2,128)} fusion(f32[128,2,400]{2,1,0:T(2,128)} %broadcast.142.clone, s32[128]{0:T(128)S(1)} %get-tuple-element.10, f32[128,400]{1,0:T(8,128)S(1)} %copy.43), kind=kCustom, calls=%fused_computation.7 | custom fusion | bytes 615424 | tf_op jit(solution)/shard_map/scatter | solution.py:95
  281.5 13.8 %all-to-all-start.4 = ((f32[128,2,400]{2,1,0:T(2,128)}), f32[128,2,400]{2,1,0:T(2,128)S(1)}, u32[]{:S(2)}, u32[]{:S(2)}) async-start(f32[128,2,400]{2,1,0:T(2,128)} %scatter_fusion.2), calls=%async_computation.4 | async-start | bytes 1048576 | tf_op jit(solution)/shard_map/all_to_all | solution.py:103
  295.3 0.1 copy.44
  295.4 0.9 broadcast.142.clone.1
  296.3 15.1 %scatter_fusion.3 = f32[128,2,400]{2,1,0:T(2,128)} fusion(f32[128,2,400]{2,1,0:T(2,128)} %broadcast.142.clone.1, s32[128]{0:T(128)S(1)} %get-tuple-element.8, f32[128,400]{1,0:T(8,128)S(1)} %copy.44), kind=kCustom, calls=%fused_computation.9 | custom fusion | bytes 615424 | tf_op jit(solution)/shard_map/scatter | solution.py:100
  311.5 15.1 %all-to-all-done.4 = f32[128,2,400]{2,1,0:T(2,128)S(1)} async-done(((f32[128,2,400]{2,1,0:T(2,128)}), f32[128,2,400]{2,1,0:T(2,128)S(1)}, u32[]{:S(2)}, u32[]{:S(2)}) %all-to-all-start.4) | async-done | bytes 409632 | tf_op jit(solution)/shard_map/all_to_all | solution.py:103
  326.6 8.6 %all-to-all-start.5 = ((f32[128,2,400]{2,1,0:T(2,128)}), f32[128,2,400]{2,1,0:T(2,128)S(1)}, u32[]{:S(2)}, u32[]{:S(2)}) async-start(f32[128,2,400]{2,1,0:T(2,128)} %scatter_fusion.3), calls=%async_computation.5 | async-start | bytes 1048576 | tf_op jit(solution)/shard_map/all_to_all | solution.py:104
  335.3 1.0 fusion.10
  336.3 2.1 convolution_add_fusion
  338.5 1.3 dynamic-slice
  340.4 0.4 reshape.171
  340.8 2.3 scatter_custom_fusion.3
  343.1 23.4 %all-to-all-done.5 = f32[128,2,400]{2,1,0:T(2,128)S(1)} async-done(((f32[128,2,400]{2,1,0:T(2,128)}), f32[128,2,400]{2,1,0:T(2,128)S(1)}, u32[]{:S(2)}, u32[]{:S(2)}) %all-to-all-start.5) | async-done | bytes 409632 | tf_op jit(solution)/shard_map/all_to_all | solution.py:104
  366.5 0.4 reshape.185
  366.9 2.5 scatter_fusion.4
  369.4 307.0 %all-reduce.6.cloned.1.call-done = f32[512,400]{1,0:T(8,128)} async-done(((f32[512,400]{1,0:T(8,128)}), f32[512,400]{1,0:T(8,128)}) %all-reduce.6.cloned.1.call-update) | async-done | bytes 819216
  676.4 1.2 scatter_custom_fusion.6
  677.6 1.0 copy-done.1
  678.7 58.2 %all-reduce.4.cloned.1.call-done = f32[512,400]{1,0:T(8,128)} async-done(((f32[512,400]{1,0:T(8,128)}), f32[512,400]{1,0:T(8,128)}) %all-reduce.4.cloned.1.call-update) | async-done | bytes 819216 | tf_op jit(solution)/shard_map/psum | solution.py:111
  736.9 1.5 multiply_reduce_fusion
  738.4 0.6 fusion.25
  739.0 0.2 divide_subtract_fusion
  739.2 1.2 copy.46
  (50 shorter events, 0.8 us)
Async XLA Ops:
  7.2 243.6 %copy-start = (f32[64,400]{1,0:T(8,128)S(1)}, f32[64,400]{1,0:T(8,128)}, u32[]{:S(2)}) copy-start(f32[64,400]{1,0:T(8,128)} %param.17) | copy-start | bytes 307204
  7.2 0.7 copy-start.9
  8.0 0.7 copy-start.12
  8.1 28.2 %copy-start.7 = (f32[512,400]{0,1:T(8,128)S(1)}, f32[512,400]{0,1:T(8,128)}, u32[]{:S(2)}) copy-start(f32[512,400]{0,1:T(8,128)} %param.9) | copy-start | bytes 2457604
  15.7 33.3 %all-to-all-start.2 = ((s32[128,1,2]{2,1,0:T(1,128)}), s32[128,1,2]{2,1,0:T(1,128)S(1)}, u32[]{:S(2)}, u32[]{:S(2)}) async-start(s32[128,1,2]{2,1,0:T(1,128)} %copy.35), calls=%async_computation.2 | async-start | bytes 131072 | tf_op jit(solution)/shard_map/all_to_all | solution.py:51
  35.2 0.7 copy-start.10
  36.7 0.7 copy-start.13
  49.1 25.4 %all-to-all-start = ((s32[128,1,2]{2,1,0:T(1,128)}), s32[128,1,2]{2,1,0:T(1,128)S(1)}, u32[]{:S(2)}, u32[]{:S(2)}) async-start(s32[128,1,2]{2,1,0:T(1,128)} %copy.33), calls=%async_computation | async-start | bytes 131072 | tf_op jit(solution)/shard_map/all_to_all | solution.py:51
  74.4 38.1 %all-to-all-start.3 = ((f32[128,2,400]{2,1,0:T(2,128)}), f32[128,2,400]{2,1,0:T(2,128)S(1)}, u32[]{:S(2)}, u32[]{:S(2)}) async-start(f32[128,2,400]{2,1,0:T(2,128)} %reshape.128), calls=%async_computation.3 | async-start | bytes 1048576 | tf_op jit(solution)/shard_map/all_to_all | solution.py:53
  83.4 37.8 %copy-start.15 = (s32[4]{0:T(128)S(1)}, s32[4]{0:T(128)}, u32[]{:S(2)}) copy-start(s32[4]{0:T(128)} %param.16) | copy-start | bytes 52
  112.6 142.3 %all-to-all-start.1 = ((f32[128,2,400]{2,1,0:T(2,128)}), f32[128,2,400]{2,1,0:T(2,128)S(1)}, u32[]{:S(2)}, u32[]{:S(2)}) async-start(f32[128,2,400]{2,1,0:T(2,128)} %reshape.114), calls=%async_computation.1 | async-start | bytes 1048576 | tf_op jit(solution)/shard_map/all_to_all | solution.py:53
  249.1 1.6 copy-start.14
  256.6 1.1 copy-start.8
  257.8 6.4 copy-start.3
  257.8 6.4 copy-start.5
  281.5 45.1 %all-to-all-start.4 = ((f32[128,2,400]{2,1,0:T(2,128)}), f32[128,2,400]{2,1,0:T(2,128)S(1)}, u32[]{:S(2)}, u32[]{:S(2)}) async-start(f32[128,2,400]{2,1,0:T(2,128)} %scatter_fusion.2), calls=%async_computation.4 | async-start | bytes 1048576 | tf_op jit(solution)/shard_map/all_to_all | solution.py:103
  311.5 23.8 %copy-start.4 = (f32[128,200]{0,1:T(8,128)S(1)}, f32[128,200]{0,1:T(8,128)}, u32[]{:S(2)}) copy-start(f32[128,200]{0,1:T(8,128)} %copy-done.3) | copy-start | bytes 307204
  311.5 23.8 %copy-start.6 = (f32[128,200]{0,1:T(8,128)S(1)}, f32[128,200]{0,1:T(8,128)}, u32[]{:S(2)}) copy-start(f32[128,200]{0,1:T(8,128)} %copy-done.5) | copy-start | bytes 307204
  326.6 39.9 %all-to-all-start.5 = ((f32[128,2,400]{2,1,0:T(2,128)}), f32[128,2,400]{2,1,0:T(2,128)S(1)}, u32[]{:S(2)}, u32[]{:S(2)}) async-start(f32[128,2,400]{2,1,0:T(2,128)} %scatter_fusion.3), calls=%async_computation.5 | async-start | bytes 1048576 | tf_op jit(solution)/shard_map/all_to_all | solution.py:104
  335.2 341.2 %all-reduce.6.cloned.1.call-start = ((), (), s32[]{:S(2)}) async-start(), calls=%async_computation.7 | async-start | bytes 2097152
  338.4 398.5 %all-reduce.4.cloned.1.call-start = ((), (), s32[]{:S(2)}) async-start(), calls=%async_computation.6 | async-start | bytes 2097152 | tf_op jit(solution)/shard_map/psum | solution.py:111
  677.6 1.0 copy-start.1
  678.7 59.7 %copy-start.11 = (f32[512]{0:T(512)S(1)}, f32[512]{0:T(512)}, u32[]{:S(2)}) copy-start(f32[512]{0:T(512)} %param.10) | copy-start | bytes 6148
  736.9 2.1 copy-start.2
Sparse Core Ops, SparseCore 0:
  339.5 336.8 all-reduce.5
  678.9 57.9 all-reduce.3
where the time goes:
time: 749 us; the launch traced here: 747 us
  waiting for transfers between devices  449 us (60%)
  blocking collectives  127 us (17%)
  starting transfers between devices  68.7 us (9%)
  local copies, waits for them, and re-layouts  67.7 us (9%)
  between operations  15.2 us (2%)
  matrix products  9.73 us (1%)
  other arithmetic  9.47 us (1%)
    unnamed x3, waiting for transfers between devices  307 us
    all_gather x1, blocking collectives, on_device(): lax.all_gather(entity_table[neg_rows], 'ent', axis=0, tiled=True)  127 us
    psum x1, waiting for transfers between devices, on_device(): total_grad = lax.psum(grad_table, 'rep')  58.2 us
    all_to_all x2, starting transfers between devices, fetch_single(): lax.all_to_all(asks, 'ent', split_axis=0, concat_axis=0, tiled=True)  31 us
    all_to_all x2, waiting for transfers between devices, fetch_single(): lax.all_to_all(found, 'ent', split_axis=0, concat_axis=0, tiled=True)  29.2 us
    all_to_all x1, waiting for transfers between devices, on_device(): lax.all_to_all(tail_buffer, 'ent', split_axis=0, concat_axis=0, tiled=True)  23.4 us
    all_to_all x2, waiting for transfers between devices, fetch_single(): lax.all_to_all(asks, 'ent', split_axis=0, concat_axis=0, tiled=True)  16.2 us
    scatter x1, local copies, waits for them, and re-layouts, on_device(): head_buffer = jnp.zeros((owners_count, capacity, width), jnp.float32).at[...  16.1 us
  transfers between devices with their start and end apart: 8, of which 7 were waited for; matrix products, arithmetic and copies ran while one was open for 6% of the time, Pallas kernels for 0%

commit v1 on v0

--- a/solution.py
+++ b/solution.py
@@ -81,7 +81,10 @@
     )
     head_back, head_recv = fetch_single(head_asks, entity_table)
     tail_back, tail_recv = fetch_single(tail_asks, entity_table)
-    negatives = lax.all_gather(entity_table[neg_rows], "ent", axis=0, tiled=True)
+    negatives = jnp.concatenate(
+        lax.all_to_all(jnp.stack([entity_table[neg_rows]] * lax.axis_size("ent")), "ent", 0, 0),
+        axis=0,
+    )
     heads = head_back[head_dest, head_slot]
     tails = tail_back[tail_dest, tail_slot]
     relation_pick = (

time: 749 us -> 702 us (0.937)
  blocking collectives: 127 us -> 0 us
  waiting for transfers between devices: 449 us -> 523 us
    all_gather x1 -> x0, blocking collectives: 127 us -> none  [on_device(): lax.all_gather(entity_table[neg_rows], 'ent', axis=0, tiled=True)]
    all_to_all x0 -> x1, waiting for transfers between devices: none -> 43.9 us  [on_device(): lax.all_to_all(jnp.stack([entity_table[neg_rows]] * lax.axis_size('ent'))...]
    all_to_all x2, waiting for transfers between devices: 29.2 us -> 59.9 us  [fetch_single(): lax.all_to_all(found, 'ent', split_axis=0, concat_axis=0, tiled=True)]
    all_to_all x0 -> x1, starting transfers between devices: none -> 8.72 us  [on_device(): lax.all_to_all(jnp.stack([entity_table[neg_rows]] * lax.axis_size('ent'))...]
  transfers between devices with their start and end apart: 8 -> 9, of which waited for: 7 -> 9; matrix products, arithmetic and copies ran while one was open for 6% -> 7% of each run, Pallas kernels for 0% -> 0%
where the time goes in v1:
time: 702 us; the launch traced here: 700 us
  waiting for transfers between devices  523 us (75%)
  starting transfers between devices  73.6 us (10%)
  local copies, waits for them, and re-layouts  68.3 us (10%)
  between operations  15.2 us (2%)
  matrix products  10.4 us (1%)
  other arithmetic  10.2 us (1%)
    unnamed x3, waiting for transfers between devices  306 us
    all_to_all x2, waiting for transfers between devices, fetch_single(): lax.all_to_all(found, 'ent', split_axis=0, concat_axis=0, tiled=True)  59.9 us
    psum x1, waiting for transfers between devices, on_device(): total_grad = lax.psum(grad_table, 'rep')  58.2 us
    all_to_all x1, waiting for transfers between devices, on_device(): lax.all_to_all(jnp.stack([entity_table[neg_rows]] * lax.axis_size('ent'))...  43.9 us
    all_to_all x2, starting transfers between devices, fetch_single(): lax.all_to_all(asks, 'ent', split_axis=0, concat_axis=0, tiled=True)  31 us
    all_to_all x1, waiting for transfers between devices, on_device(): lax.all_to_all(tail_buffer, 'ent', split_axis=0, concat_axis=0, tiled=True)  23.1 us
    all_to_all x2, waiting for transfers between devices, fetch_single(): lax.all_to_all(asks, 'ent', split_axis=0, concat_axis=0, tiled=True)  16.3 us
    scatter x1, local copies, waits for them, and re-layouts, on_device(): head_buffer = jnp.zeros((owners_count, capacity, width), jnp.float32).at[...  15.9 us
  transfers between devices with their start and end apart: 9, of which 9 were waited for; matrix products, arithmetic and copies ran while one was open for 7% of the time, Pallas kernels for 0%

profile of v1, /device:TPU:8, one launch (start us, length us, event | category | flops | bytes accessed | tf_op | source)
XLA Modules:
  0.0 700.4 jit_solution(14295764036542616509)
XLA Ops:
  7.2 0.7 copy-done.11
  8.0 0.2 reduce_window_sum.18
  8.1 0.2 select_reduce_fusion
  8.4 0.3 copy-done.14
  8.6 6.4 scatter_fusion.1
  15.0 0.7 copy.35
  15.7 19.5 %all-to-all-start.2 = ((s32[128,1,2]{2,1,0:T(1,128)}), s32[128,1,2]{2,1,0:T(1,128)S(1)}, u32[]{:S(2)}, u32[]{:S(2)}) async-start(s32[128,1,2]{2,1,0:T(1,128)} %copy.35), calls=%async_computation.2 | async-start | bytes 131072 | tf_op jit(solution)/shard_map/all_to_all | solution.py:51
  35.3 0.6 copy-done.12
  36.0 0.2 reduce_window_sum.17
  36.2 0.2 select_reduce_fusion.1
  36.4 0.3 copy.45
  36.7 0.6 copy-done.15
  37.4 6.4 scatter_fusion
  43.7 0.7 copy.33
  44.5 4.6 all-to-all-done.2
  49.1 11.5 %all-to-all-start = ((s32[128,1,2]{2,1,0:T(1,128)}), s32[128,1,2]{2,1,0:T(1,128)S(1)}, u32[]{:S(2)}, u32[]{:S(2)}) async-start(s32[128,1,2]{2,1,0:T(1,128)} %copy.33), calls=%async_computation | async-start | bytes 131072 | tf_op jit(solution)/shard_map/all_to_all | solution.py:51
  60.8 1.0 gather_fusion.2
  61.7 1.1 reshape.134
  62.9 11.7 %all-to-all-done = s32[128,1,2]{2,1,0:T(1,128)S(1)} async-done(((s32[128,1,2]{2,1,0:T(1,128)}), s32[128,1,2]{2,1,0:T(1,128)S(1)}, u32[]{:S(2)}, u32[]{:S(2)}) %all-to-all-start) | async-done | bytes 1056 | tf_op jit(solution)/shard_map/all_to_all | solution.py:51
  74.6 6.6 all-to-all-start.3
  81.3 1.0 gather_fusion
  82.3 1.1 reshape.120
  83.5 29.2 %all-to-all-done.3 = f32[128,2,400]{2,1,0:T(2,128)S(1)} async-done(((f32[128,2,400]{2,1,0:T(2,128)}), f32[128,2,400]{2,1,0:T(2,128)S(1)}, u32[]{:S(2)}, u32[]{:S(2)}) %all-to-all-start.3) | async-done | bytes 409632 | tf_op jit(solution)/shard_map/all_to_all | solution.py:53
  112.6 8.6 %all-to-all-start.1 = ((f32[128,2,400]{2,1,0:T(2,128)}), f32[128,2,400]{2,1,0:T(2,128)S(1)}, u32[]{:S(2)}, u32[]{:S(2)}) async-start(f32[128,2,400]{2,1,0:T(2,128)} %reshape.120), calls=%async_computation.1 | async-start | bytes 1048576 | tf_op jit(solution)/shard_map/all_to_all | solution.py:53
  121.3 0.6 gather_fusion.4
  121.8 30.7 %all-to-all-done.1 = f32[128,2,400]{2,1,0:T(2,128)S(1)} async-done(((f32[128,2,400]{2,1,0:T(2,128)}), f32[128,2,400]{2,1,0:T(2,128)S(1)}, u32[]{:S(2)}, u32[]{:S(2)}) %all-to-all-start.1) | async-done | bytes 409632 | tf_op jit(solution)/shard_map/all_to_all | solution.py:53
  152.6 1.1 stack.2
  153.7 8.7 %all-to-all-start.4 = ((f32[128,4,400]{2,1,0:T(4,128)}), f32[128,4,400]{2,1,0:T(4,128)S(1)}, u32[]{:S(2)}, u32[]{:S(2)}) async-start(f32[128,4,400]{2,1,0:T(4,128)} %stack.2), calls=%async_computation.4 | async-start | bytes 2097152 | tf_op jit(solution)/shard_map/all_to_all | solution.py:85
  162.4 1.1 fusion.13
  163.5 1.8 gather_fusion.3
  165.3 1.1 fusion.28
  166.5 0.7 copy.47
  167.2 1.8 gather_fusion.1
  169.0 1.1 copy.39
  170.1 0.8 multiply_subtract_fusion.3
  171.0 43.9 %all-to-all-done.4 = f32[128,4,400]{2,1,0:T(4,128)S(1)} async-done(((f32[128,4,400]{2,1,0:T(4,128)}), f32[128,4,400]{2,1,0:T(4,128)S(1)}, u32[]{:S(2)}, u32[]{:S(2)}) %all-to-all-start.4) | async-done | bytes 819232 | tf_op jit(solution)/shard_map/all_to_all | solution.py:85
  214.9 0.4 reshape.118
  215.3 1.3 fusion.7
  216.6 1.8 fusion.30
  218.4 1.3 fusion.4
  219.8 1.8 fusion.29
  221.9 0.9 broadcast.144.clone
  222.8 15.9 %scatter_fusion.2 = f32[128,2,400]{2,1,0:T(2,128)} fusion(f32[128,2,400]{2,1,0:T(2,128)} %broadcast.144.clone, s32[128]{0:T(128)S(1)} %get-tuple-element.10, f32[128,400]{1,0:T(8,128)S(1)} %copy.43), kind=kCustom, calls=%fused_computation.7 | custom fusion | bytes 615424 | tf_op jit(solution)/shard_map/scatter | solution.py:98
  238.7 9.5 %all-to-all-start.5 = ((f32[128,2,400]{2,1,0:T(2,128)}), f32[128,2,400]{2,1,0:T(2,128)S(1)}, u32[]{:S(2)}, u32[]{:S(2)}) async-start(f32[128,2,400]{2,1,0:T(2,128)} %scatter_fusion.2), calls=%async_computation.5 | async-start | bytes 1048576 | tf_op jit(solution)/shard_map/all_to_all | solution.py:106
  248.4 0.9 broadcast.144.clone.1
  249.3 15.1 %scatter_fusion.3 = f32[128,2,400]{2,1,0:T(2,128)} fusion(f32[128,2,400]{2,1,0:T(2,128)} %broadcast.144.clone.1, s32[128]{0:T(128)S(1)} %get-tuple-element.8, f32[128,400]{1,0:T(8,128)S(1)} %copy.44), kind=kCustom, calls=%fused_computation.9 | custom fusion | bytes 615424 | tf_op jit(solution)/shard_map/scatter | solution.py:103
  264.4 15.1 %all-to-all-done.5 = f32[128,2,400]{2,1,0:T(2,128)S(1)} async-done(((f32[128,2,400]{2,1,0:T(2,128)}), f32[128,2,400]{2,1,0:T(2,128)S(1)}, u32[]{:S(2)}, u32[]{:S(2)}) %all-to-all-start.5) | async-done | bytes 409632 | tf_op jit(solution)/shard_map/all_to_all | solution.py:106
  279.6 9.1 %all-to-all-start.6 = ((f32[128,2,400]{2,1,0:T(2,128)}), f32[128,2,400]{2,1,0:T(2,128)}, u32[]{:S(2)}, u32[]{:S(2)}) async-start(f32[128,2,400]{2,1,0:T(2,128)} %scatter_fusion.3), calls=%async_computation.6 | async-start | bytes 1048576 | tf_op jit(solution)/shard_map/all_to_all | solution.py:107
  288.7 1.0 fusion.10
  289.7 2.1 convolution_add_fusion
  291.9 1.3 dynamic-slice
  293.8 0.4 reshape.177
  294.2 2.3 scatter_custom_fusion.3
  296.5 23.1 %all-to-all-done.6 = f32[128,2,400]{2,1,0:T(2,128)} async-done(((f32[128,2,400]{2,1,0:T(2,128)}), f32[128,2,400]{2,1,0:T(2,128)}, u32[]{:S(2)}, u32[]{:S(2)}) %all-to-all-start.6) | async-done | bytes 409632 | tf_op jit(solution)/shard_map/all_to_all | solution.py:107
  319.6 1.4 reshape.191
  321.0 2.5 scatter_fusion.4
  323.5 306.0 %all-reduce.6.cloned.1.call-done = f32[512,400]{1,0:T(8,128)} async-done(((f32[512,400]{1,0:T(8,128)}), f32[512,400]{1,0:T(8,128)}) %all-reduce.6.cloned.1.call-update) | async-done | bytes 819216
  629.6 1.2 scatter_custom_fusion.6
  630.8 1.0 copy-done.1
  631.8 58.2 %all-reduce.4.cloned.1.call-done = f32[512,400]{1,0:T(8,128)} async-done(((f32[512,400]{1,0:T(8,128)}), f32[512,400]{1,0:T(8,128)}) %all-reduce.4.cloned.1.call-update) | async-done | bytes 819216 | tf_op jit(solution)/shard_map/psum | solution.py:114
  690.1 1.5 multiply_reduce_fusion
  691.5 0.6 fusion.25
  692.1 0.2 divide_subtract_fusion
  692.3 1.2 copy.46
  (56 shorter events, 1.3 us)
Async XLA Ops:
  7.2 155.2 %copy-start = (f32[64,400]{1,0:T(8,128)S(1)}, f32[64,400]{1,0:T(8,128)}, u32[]{:S(2)}) copy-start(f32[64,400]{1,0:T(8,128)} %param.17) | copy-start | bytes 307204
  7.2 0.7 copy-start.11
  8.0 0.7 copy-start.14
  8.1 28.2 %copy-start.9 = (f32[512,400]{0,1:T(8,128)S(1)}, f32[512,400]{0,1:T(8,128)}, u32[]{:S(2)}) copy-start(f32[512,400]{0,1:T(8,128)} %param.9) | copy-start | bytes 2457604
  15.7 33.3 %all-to-all-start.2 = ((s32[128,1,2]{2,1,0:T(1,128)}), s32[128,1,2]{2,1,0:T(1,128)S(1)}, u32[]{:S(2)}, u32[]{:S(2)}) async-start(s32[128,1,2]{2,1,0:T(1,128)} %copy.35), calls=%async_computation.2 | async-start | bytes 131072 | tf_op jit(solution)/shard_map/all_to_all | solution.py:51
  35.2 0.7 copy-start.12
  36.7 0.7 copy-start.15
  49.1 25.5 %all-to-all-start = ((s32[128,1,2]{2,1,0:T(1,128)}), s32[128,1,2]{2,1,0:T(1,128)S(1)}, u32[]{:S(2)}, u32[]{:S(2)}) async-start(s32[128,1,2]{2,1,0:T(1,128)} %copy.33), calls=%async_computation | async-start | bytes 131072 | tf_op jit(solution)/shard_map/all_to_all | solution.py:51
  74.6 38.1 %all-to-all-start.3 = ((f32[128,2,400]{2,1,0:T(2,128)}), f32[128,2,400]{2,1,0:T(2,128)S(1)}, u32[]{:S(2)}, u32[]{:S(2)}) async-start(f32[128,2,400]{2,1,0:T(2,128)} %reshape.134), calls=%async_computation.3 | async-start | bytes 1048576 | tf_op jit(solution)/shard_map/all_to_all | solution.py:53
  83.5 37.8 %copy-start.17 = (s32[4]{0:T(128)S(1)}, s32[4]{0:T(128)}, u32[]{:S(2)}) copy-start(s32[4]{0:T(128)} %param.16) | copy-start | bytes 52
  112.6 39.9 %all-to-all-start.1 = ((f32[128,2,400]{2,1,0:T(2,128)}), f32[128,2,400]{2,1,0:T(2,128)S(1)}, u32[]{:S(2)}, u32[]{:S(2)}) async-start(f32[128,2,400]{2,1,0:T(2,128)} %reshape.120), calls=%async_computation.1 | async-start | bytes 1048576 | tf_op jit(solution)/shard_map/all_to_all | solution.py:53
  153.7 8.7 %copy-start.16 = (s32[128]{0:T(128)S(1)}, s32[128]{0:T(128)}, u32[]{:S(2)}) copy-start(s32[128]{0:T(128)} %param.13) | copy-start | bytes 1540
  153.7 61.2 %all-to-all-start.4 = ((f32[128,4,400]{2,1,0:T(4,128)}), f32[128,4,400]{2,1,0:T(4,128)S(1)}, u32[]{:S(2)}, u32[]{:S(2)}) async-start(f32[128,4,400]{2,1,0:T(4,128)} %stack.2), calls=%async_computation.4 | async-start | bytes 2097152 | tf_op jit(solution)/shard_map/all_to_all | solution.py:85
  169.0 1.1 copy-start.3
  169.0 1.1 copy-start.10
  216.6 1.8 copy-start.5
  216.6 1.8 copy-start.7
  219.8 1.8 copy-start.4
  238.7 40.9 %all-to-all-start.5 = ((f32[128,2,400]{2,1,0:T(2,128)}), f32[128,2,400]{2,1,0:T(2,128)S(1)}, u32[]{:S(2)}, u32[]{:S(2)}) async-start(f32[128,2,400]{2,1,0:T(2,128)} %scatter_fusion.2), calls=%async_computation.5 | async-start | bytes 1048576 | tf_op jit(solution)/shard_map/all_to_all | solution.py:106
  264.4 24.2 %copy-start.6 = (f32[128,200]{0,1:T(8,128)S(1)}, f32[128,200]{0,1:T(8,128)}, u32[]{:S(2)}) copy-start(f32[128,200]{0,1:T(8,128)} %get-tuple-element.24) | copy-start | bytes 307204
  264.4 24.2 %copy-start.8 = (f32[128,200]{0,1:T(8,128)S(1)}, f32[128,200]{0,1:T(8,128)}, u32[]{:S(2)}) copy-start(f32[128,200]{0,1:T(8,128)} %get-tuple-element.25) | copy-start | bytes 307204
  279.6 40.0 %all-to-all-start.6 = ((f32[128,2,400]{2,1,0:T(2,128)}), f32[128,2,400]{2,1,0:T(2,128)}, u32[]{:S(2)}, u32[]{:S(2)}) async-start(f32[128,2,400]{2,1,0:T(2,128)} %scatter_fusion.3), calls=%async_computation.6 | async-start | bytes 1048576 | tf_op jit(solution)/shard_map/all_to_all | solution.py:107
  288.6 340.9 %all-reduce.6.cloned.1.call-start = ((), (), s32[]{:S(2)}) async-start(), calls=%async_computation.8 | async-start | bytes 2097152
  291.8 398.2 %all-reduce.4.cloned.1.call-start = ((), (), s32[]{:S(2)}) async-start(), calls=%async_computation.7 | async-start | bytes 2097152 | tf_op jit(solution)/shard_map/psum | solution.py:114
  630.8 1.0 copy-start.1
  631.8 59.7 %copy-start.13 = (f32[512]{0:T(512)S(1)}, f32[512]{0:T(512)}, u32[]{:S(2)}) copy-start(f32[512]{0:T(512)} %param.10) | copy-start | bytes 6148
  690.1 2.1 copy-start.2
Sparse Core Ops, SparseCore 0:
  292.9 336.5 all-reduce.5
  632.0 57.9 all-reduce.3
